TPU v7x, 512 devices: a whole 4x8x8 slice. The times are simulated.
512 devices in a mesh: hst: 128 (over z, y, core), local: 4 (over x).
Axes of the slice: x: 4, y: 8, z: 8, core: 2. Of those that a mesh axis runs over, the one named last changes fastest.
Arguments:
- grads: bfloat16 [128, 4, 16, 49152], P('hst', 'local'), may hold values from -1.25 to 1.25
- master: float32 [16, 49152], P('local', 'hst'), may hold values from -3 to 3
- moment_one: float32 [16, 49152], P('local', 'hst'), may hold values from -3 to 3
- moment_two: float32 [16, 49152], P('local', 'hst'), may hold values from 0.01 to 2
Outputs:
- grad_total: float32 [16, 49152], P('local', 'hst')
- new_master: float32 [16, 49152], P('local', 'hst')
- new_one: float32 [16, 49152], P('local', 'hst')
- new_two: float32 [16, 49152], P('local', 'hst')
- secondary: bfloat16 [16, 49152], P('local')
All inputs are finite; a program needn't handle non-finite values.
Results may differ from a plain program's by a relative error of at most 0.001.
Values may be sent and summed in bfloat16 or wider, within the bound.
A program may use at most 64 MiB of HBM per device.

v0:
```python
import jax
import jax.numpy as jnp
from jax import lax
from jax.sharding import PartitionSpec as P

beta_one = 0.9
beta_two = 0.95
learn_rate = 0.02
decay_rate = 0.1
epsilon = 1e-08
correct_one = 1.0 - (0.9**50) ** 2
correct_two = 1.0 - (0.95**50) ** 2


def local(grads, master, moment_one, moment_two):
    local_count = lax.axis_size("local")
    host_count = lax.axis_size("hst")
    gradient = grads[0, 0]
    total_rows = gradient.shape[0]
    total_cols = gradient.shape[1]
    row_block = total_rows // local_count
    col_block = total_cols // host_count
    pieces = lax.all_to_all(
        gradient.reshape(local_count, row_block, total_cols),
        "local",
        split_axis=0,
        concat_axis=0,
        tiled=True,
    )
    partial_sum = jnp.sum(pieces.astype(jnp.float32), axis=0)
    arrived = lax.all_to_all(
        partial_sum.reshape(row_block, host_count, col_block),
        "hst",
        split_axis=1,
        concat_axis=1,
        tiled=True,
    )
    grad_total = jnp.sum(arrived, axis=1)
    new_one = beta_one * moment_one + (1.0 - beta_one) * grad_total
    new_two = beta_two * moment_two + (1.0 - beta_two) * grad_total * grad_total
    update = new_one / correct_one / (jnp.sqrt(new_two / correct_two) + epsilon)
    new_master = master - learn_rate * (update + decay_rate * master)
    secondary = lax.all_gather(new_master.astype(jnp.bfloat16), "hst", axis=1, tiled=True)
    return (grad_total, new_master, new_one, new_two, secondary)


def solution(mesh):
    return jax.shard_map(
        local,
        mesh=mesh,
        in_specs=(
            P("hst", "local", None, None),
            P("local", "hst"),
            P("local", "hst"),
            P("local", "hst"),
        ),
        out_specs=(
            P("local", "hst"),
            P("local", "hst"),
            P("local", "hst"),
            P("local", "hst"),
            P("local", None),
        ),
        check_vma=False,
    )
```

profile of v0, /device:TPU:1, one launch (start us, length us, event | category | flops | bytes accessed | tf_op | source)
XLA Modules:
  0.0 122.6 jit_solution(15280396725466493104)
XLA Ops:
  0.6 1.7 %reshape_squeeze.3 = bf16[4,4,49152]{2,1,0:T(4,128)(2,1)S(1)} reshape(bf16[1,1,16,49152]{3,2,1,0:T(8,128)(2,1)} %param.4) | data formatting | bytes 3145728 | tf_op jit(solution)/shard_map/reshape;squeeze | solution.py:24
  2.4 20.8 %all_to_all.10 = bf16[4,4,49152]{2,1,0:T(4,128)(2,1)S(1)} all-to-all(bf16[4,4,49152]{2,1,0:T(4,128)(2,1)S(1)} %reshape_squeeze.3), channel_id=1, replica_groups=mesh['hst'=128,'local'=4] {'local'}, dimensions={0} | all-to-all | bytes 3145728 | tf_op jit(solution)/shard_map/all_to_all | solution.py:23
  23.2 0.8 convert_reduce_fusion
  24.0 0.0 copy-start.1
  24.0 0.0 copy-start.2
  24.0 0.0 copy-start.3
  24.0 48.3 %all_to_all.11 = f32[4,128,384]{2,0,1:T(4,128)S(1)} all-to-all(f32[4,128,384]{2,0,1:T(4,128)S(1)} %bitcast.3), channel_id=1, replica_groups=mesh['hst'=128,'local'=4] {'hst'}, dimensions={1} | all-to-all | bytes 1572864 | tf_op jit(solution)/shard_map/all_to_all | solution.py:31
  72.3 0.2 reduce_sum.19
  72.5 0.0 copy-done.1
  72.5 0.0 copy-done.2
  72.5 0.0 copy-done.3
  72.5 0.0 copy-start
  72.5 0.6 fusion.1
  73.1 48.7 %all_gather.3 = bf16[4,49152]{1,0:T(4,128)(2,1)S(1)} all-gather(bf16[4,384]{1,0:T(4,128)(2,1)S(1)} %get-tuple-element.5), channel_id=1, replica_groups=mesh['hst'=128,'local'=4] {'hst'}, dimensions={1}, use_global_device_ids=true | all-gather | bytes 396288 | tf_op jit(solution)/shard_map/all_gather | solution.py:43
  121.8 0.7 copy.10
  122.6 0.0 copy-done
Async XLA Ops:
  24.0 48.5 %copy-start.1 = (f32[4,384]{1,0:T(4,128)S(1)}, f32[4,384]{1,0:T(4,128)}, u32[]{:S(2)}) copy-start(f32[4,384]{1,0:T(4,128)} %param.5) | copy-start | bytes 18436
  24.0 48.5 %copy-start.2 = (f32[4,384]{1,0:T(4,128)S(1)}, f32[4,384]{1,0:T(4,128)}, u32[]{:S(2)}) copy-start(f32[4,384]{1,0:T(4,128)} %param.6) | copy-start | bytes 18436
  24.0 48.5 %copy-start.3 = (f32[4,384]{1,0:T(4,128)S(1)}, f32[4,384]{1,0:T(4,128)}, u32[]{:S(2)}) copy-start(f32[4,384]{1,0:T(4,128)} %param.7) | copy-start | bytes 18436
  72.5 50.1 %copy-start = (f32[4,384]{1,0:T(4,128)}, f32[4,384]{1,0:T(4,128)S(1)}, u32[]{:S(2)}) copy-start(f32[4,384]{1,0:T(4,128)S(1)} %reduce_sum.19) | copy-start | bytes 18436
where the time goes:
time: 123 us
  blocking collectives  118 us (96%)
  local copies, waits for them, and re-layouts  2.5 us (2%)
  other arithmetic  1.59 us (1%)
    all_gather x1, blocking collectives, local(): lax.all_gather(new_master.astype(jnp.bfloat16), 'hst', axis=1, tiled=True)  48.7 us
    all_to_all x1, blocking collectives, local(): lax.all_to_all(partial_sum.reshape(row_block, host_count, col_block), 'hs...  48.3 us
    all_to_all x1, blocking collectives, local(): lax.all_to_all(gradient.reshape(local_count, row_block, total_cols), 'loc...  20.8 us

commit v1 on v0

--- a/solution.py
+++ b/solution.py
@@ -40,7 +40,12 @@
     new_two = beta_two * moment_two + (1.0 - beta_two) * grad_total * grad_total
     update = new_one / correct_one / (jnp.sqrt(new_two / correct_two) + epsilon)
     new_master = master - learn_rate * (update + decay_rate * master)
-    secondary = lax.all_gather(new_master.astype(jnp.bfloat16), "hst", axis=1, tiled=True)
+    secondary = jnp.concatenate(
+        lax.all_to_all(
+            jnp.stack([new_master.astype(jnp.bfloat16)] * lax.axis_size("hst")), "hst", 0, 0
+        ),
+        axis=1,
+    )
     return (grad_total, new_master, new_one, new_two, secondary)
 
 

time: 123 us -> 97.5 us (0.79)
  blocking collectives: 118 us -> 92.4 us
    all_gather x1 -> x0, blocking collectives: 48.7 us -> none  [local(): lax.all_gather(new_master.astype(jnp.bfloat16), 'hst', axis=1, tiled=True)]
    all_to_all x0 -> x1, blocking collectives: none -> 23.3 us  [local(): lax.all_to_all(jnp.stack([new_master.astype(jnp.bfloat16)] * lax.axis_siz...]
where the time goes in v1:
time: 97.5 us; the launch traced here: 97.3 us
  blocking collectives  92.4 us (95%)
  local copies, waits for them, and re-layouts  2.6 us (3%)
  other arithmetic  1.59 us (2%)
    all_to_all x1, blocking collectives, local(): lax.all_to_all(partial_sum.reshape(row_block, host_count, col_block), 'hs...  48.3 us
    all_to_all x1, blocking collectives, local(): lax.all_to_all(jnp.stack([new_master.astype(jnp.bfloat16)] * lax.axis_siz...  23.3 us
    all_to_all x1, blocking collectives, local(): lax.all_to_all(gradient.reshape(local_count, row_block, total_cols), 'loc...  20.8 us

profile of v1, /device:TPU:1, one launch (start us, length us, event | category | flops | bytes accessed | tf_op | source)
XLA Modules:
  0.0 97.3 jit_solution(17574983711169281757)
XLA Ops:
  0.6 1.7 %reshape_squeeze.3 = bf16[4,4,49152]{2,1,0:T(4,128)(2,1)S(1)} reshape(bf16[1,1,16,49152]{3,2,1,0:T(8,128)(2,1)} %param.4) | data formatting | bytes 3145728 | tf_op jit(solution)/shard_map/reshape;squeeze | solution.py:24
  2.4 20.8 %all_to_all.15 = bf16[4,4,49152]{2,1,0:T(4,128)(2,1)S(1)} all-to-all(bf16[4,4,49152]{2,1,0:T(4,128)(2,1)S(1)} %reshape_squeeze.3), channel_id=1, replica_groups=mesh['hst'=128,'local'=4] {'local'}, dimensions={0} | all-to-all | bytes 3145728 | tf_op jit(solution)/shard_map/all_to_all | solution.py:23
  23.2 0.8 convert_reduce_fusion
  24.0 0.0 copy-start.1
  24.0 0.0 copy-start.2
  24.0 0.0 copy-start.3
  24.0 48.3 %all_to_all.16 = f32[4,128,384]{2,0,1:T(4,128)S(1)} all-to-all(f32[4,128,384]{2,0,1:T(4,128)S(1)} %bitcast.6), channel_id=1, replica_groups=mesh['hst'=128,'local'=4] {'hst'}, dimensions={1} | all-to-all | bytes 1572864 | tf_op jit(solution)/shard_map/all_to_all | solution.py:31
  72.3 0.2 reduce_sum.19
  72.5 0.0 copy-done.1
  72.5 0.0 copy-done.2
  72.5 0.0 copy-done.3
  72.5 0.0 copy-start
  72.5 0.6 fusion.1
  73.1 0.1 stack.2
  73.2 23.3 %all_to_all.17 = bf16[128,4,384]{2,1,0:T(4,128)(2,1)S(1)} all-to-all(bf16[128,4,384]{2,1,0:T(4,128)(2,1)S(1)} %stack.2), channel_id=1, replica_groups=mesh['hst'=128,'local'=4] {'hst'}, dimensions={0} | all-to-all | bytes 786432 | tf_op jit(solution)/shard_map/all_to_all | solution.py:44
  96.5 0.7 copy.10
  97.3 0.0 copy-done
Async XLA Ops:
  24.0 48.5 %copy-start.1 = (f32[4,384]{1,0:T(4,128)S(1)}, f32[4,384]{1,0:T(4,128)}, u32[]{:S(2)}) copy-start(f32[4,384]{1,0:T(4,128)} %param.5) | copy-start | bytes 18436
  24.0 48.5 %copy-start.2 = (f32[4,384]{1,0:T(4,128)S(1)}, f32[4,384]{1,0:T(4,128)}, u32[]{:S(2)}) copy-start(f32[4,384]{1,0:T(4,128)} %param.6) | copy-start | bytes 18436
  24.0 48.5 %copy-start.3 = (f32[4,384]{1,0:T(4,128)S(1)}, f32[4,384]{1,0:T(4,128)}, u32[]{:S(2)}) copy-start(f32[4,384]{1,0:T(4,128)} %param.7) | copy-start | bytes 18436
  72.5 24.8 %copy-start = (f32[4,384]{1,0:T(4,128)}, f32[4,384]{1,0:T(4,128)S(1)}, u32[]{:S(2)}) copy-start(f32[4,384]{1,0:T(4,128)S(1)} %reduce_sum.19) | copy-start | bytes 18436
